TPU v7x, 128 devices: a whole 4x4x4 slice. The times are simulated.
128 devices in a mesh: gx: 8 (over x_lo, z), gy: 16 (over x_hi, y, core).
Axes of the slice: x: 4 (x_hi: 2, x_lo: 2; x = x_hi * 2 + x_lo), y: 4, z: 4, core: 2. Of those that a mesh axis runs over, the one named last changes fastest.
Arguments:
- scalars: float32 [4, 64, 128, 2048], P(None, None, 'gx', 'gy'), may hold values from -6 to 6
- winds: float32 [2, 64, 128, 2048], P(None, None, 'gx', 'gy'), may hold values from -0.6 to 0.6
- map_factor: float32 [128, 2048], P('gx', 'gy'), may hold values from 0.7 to 1.3
- urban_counts: int32 [128], P(('gx', 'gy')), may hold values from 256 to 1024, as said below
- urban_cols: int32 [131072], P(('gx', 'gy')), may hold values from 0 to 2047, as said below
- street_class: int32 [131072], P(('gx', 'gy')), may hold values from 0 to 9
- area_table: float32 [10, 10], replicated, may hold values from 0.2 to 1
- wall_temp: float32 [10, 131072], P(None, ('gx', 'gy')), may hold values from -6 to 6
- indoor_temp: float32 [131072], P(('gx', 'gy')), may hold values from -6 to 6
Outputs:
- scalars_out: float32 [4, 64, 128, 2048], P(None, None, 'gx', 'gy')
- wall_out: float32 [10, 131072], P(None, ('gx', 'gy'))
- indoor_out: float32 [131072], P(('gx', 'gy'))
Inputs may be any that keep to these rules, and one draw needn't show every extreme that they name: `urban_counts`: some tile has exactly 1024 live urban columns. `urban_cols`: the 1024 entries of each tile are distinct cells of that tile, numbered x * 128 + y within it.
All inputs are finite; a program needn't handle non-finite values.
Results may differ from a plain program's by a relative error of at most 0.000056.
Values sent between devices are 32-bit elements; how exact they have to be, the bound alone decides.
A program may use at most 192 MiB of HBM per device.

v0:
```python
import jax
import jax.numpy as jnp
from jax import lax
from jax.experimental import pallas as pl
from jax.experimental.pallas import tpu as pltpu
from jax.sharding import PartitionSpec as P

MESH = pl.DeviceIdType.MESH
UL = 10
NWL = 10
LOW = 16

heat_coef = 0.5
wall_coef = 0.05
conduct = 0.3
inner_coef = 0.2
room_coef = 0.1
flux_coef = 0.5

CX = 16
LANES = 128
NSC = 4
LEV = 64
ROWS = 8
CHUNKS = LEV // ROWS
H = 3
EDGE_X = (0, 1, 2, 13, 14, 15)
INNER_X = tuple(range(3, 13))


def roll(value, shift):
    return pltpu.roll(value, shift % LANES, 1)


def flux_terms(m3, m2, m1, q, p1, p2, speed):
    even = 37.0 * (m1 + q) - 8.0 * (m2 + p1) + (m3 + p2)
    odd = (p2 - m3) - 5.0 * (p1 - m2) + 10.0 * (q - m1)
    return speed * even - jnp.abs(speed) * odd


def step_kernel(
    scal, wind, mapf, out,
    field, windx, windy, facex, facey, facee, square, own, give_n, give_s, got_s, got_n, result, wpack, wgot, mapbuf,
    load_s, load_w, load_m, sx, rx, sy, ry, swx, rwx, swy, rwy, store_o,
):
    gx, gy = lax.axis_index("gx"), lax.axis_index("gy")
    nx, ny = lax.axis_size("gx"), lax.axis_size("gy")
    east, west = {"gx": lax.rem(gx + 1, nx)}, {"gx": lax.rem(gx + nx - 1, nx)}
    north, south = {"gy": lax.rem(gy + 1, ny)}, {"gy": lax.rem(gy + ny - 1, ny)}

    barrier = pltpu.get_barrier_semaphore()
    for device in (east, west, north, south):
        pl.semaphore_signal(barrier, inc=1, device_id=device, device_id_type=MESH)

    def load_scalar(s, x):
        return pltpu.make_async_copy(scal.at[s, :, x, :], field.at[0, H + x, s], load_s.at[s, x])

    def load_wind(which, x):
        target = windx.at[1 + x] if which == 0 else windy.at[x]
        return pltpu.make_async_copy(wind.at[which, :, x, :], target, load_w.at[which, x])

    load_map = pltpu.make_async_copy(mapf, mapbuf, load_m)
    for s in range(NSC):
        for x in EDGE_X:
            load_scalar(s, x).start()
    load_wind(0, 0).start()
    load_wind(0, CX - 1).start()
    for x in range(CX):
        load_wind(1, x).start()
    for s in range(NSC):
        for x in INNER_X:
            load_scalar(s, x).start()
    for x in range(1, CX - 1):
        load_wind(0, x).start()
    load_map.start()

    def remote(src, dst, send, recv, device):
        return pltpu.make_async_remote_copy(
            src_ref=src, dst_ref=dst, send_sem=send, recv_sem=recv, device_id=device, device_id_type=MESH
        )

    def rows_of(k):
        return pl.ds(pl.multiple_of(k * ROWS, ROWS), ROWS)

    def x_copies(sec, k):
        rows = rows_of(k)
        return (
            remote(field.at[sec, pl.ds(CX, H), :, rows, :], field.at[sec, pl.ds(0, H), :, rows, :],
                   sx.at[sec, k, 0], rx.at[sec, k, 0], east),
            remote(field.at[sec, pl.ds(H, H), :, rows, :], field.at[sec, pl.ds(CX + H, H), :, rows, :],
                   sx.at[sec, k, 1], rx.at[sec, k, 1], west),
        )

    def y_copies(sec, k):
        return (
            remote(give_n.at[sec, k], got_s.at[sec, k], sy.at[sec, k, 0], ry.at[sec, k, 0], north),
            remote(give_s.at[sec, k], got_n.at[sec, k], sy.at[sec, k, 1], ry.at[sec, k, 1], south),
        )

    wx_copies = (
        remote(windx.at[CX], windx.at[0], swx.at[0], rwx.at[0], east),
        remote(windx.at[1], windx.at[CX + 1], swx.at[1], rwx.at[1], west),
    )
    wy_copies = (
        remote(wpack.at[0], wgot.at[0], swy.at[0], rwy.at[0], north),
        remote(wpack.at[1], wgot.at[1], swy.at[1], rwy.at[1], south),
    )

    for s in range(NSC):
        for x in EDGE_X:
            load_scalar(s, x).wait()
    load_wind(0, 0).wait()
    load_wind(0, CX - 1).wait()
    pl.semaphore_wait(barrier, 4)
    for copy in wx_copies:
        copy.start()

    def send_first(k, carry):
        for copy in x_copies(0, k):
            copy.start()
        return carry

    lax.fori_loop(0, CHUNKS, send_first, 0)

    lane = lax.broadcasted_iota(jnp.int32, (ROWS, LANES), 1)
    slot = lane // 8
    inside = lane % 8
    low = inside < 3

    def pack_send(sec, k, pair, first, second):
        give_n[sec, k, pair] = jnp.where(low, first, roll(second, 3))
        give_s[sec, k, pair] = jnp.where(low, roll(first, -3), second)

    for x in range(CX):
        load_wind(1, x).wait()
    to_n = jnp.zeros((ROWS, LANES), jnp.float32)
    to_s = jnp.zeros((ROWS, LANES), jnp.float32)
    for k in range(CHUNKS):
        packed = jnp.zeros((ROWS, LANES), jnp.float32)
        for x in range(CX):
            packed = jnp.where(slot == x, roll(windy[x, pl.ds(k * ROWS, ROWS), :], 8 * x + 3), packed)
        to_n = jnp.where(inside == k, roll(packed, k - 2), to_n)
        to_s = jnp.where(inside == k, roll(packed, k - 3), to_s)
        facee[pl.ds(k * ROWS, ROWS), :] = packed
    wpack[0] = to_n
    wpack[1] = to_s
    for copy in wy_copies:
        copy.start()

    for s in range(NSC):
        for x in INNER_X:
            load_scalar(s, x).wait()

    def pack_first(k, carry):
        rows = rows_of(k)
        for pair in range(2):
            packs = []
            for s in (2 * pair, 2 * pair + 1):
                packed = jnp.zeros((ROWS, LANES), jnp.float32)
                for x in range(CX):
                    packed = jnp.where(slot == x, roll(field[0, H + x, s, rows, :], 8 * x + 3), packed)
                own[0, s, rows, :] = packed
                packs.append(packed)
            pack_send(0, k, pair, *packs)
        for copy in y_copies(0, k):
            copy.start()
        return carry

    lax.fori_loop(0, CHUNKS, pack_first, 0)

    load_map.wait()
    for x in range(CX):
        factor = jnp.broadcast_to(mapbuf[pl.ds(x, 1), :], (ROWS, LANES))
        minus = factor * factor
        square[0, x] = minus * (1.0 / 3.0)
        square[1, x] = minus * 0.5
        square[2, x] = minus
    for x in range(1, CX - 1):
        load_wind(0, x).wait()
    for copy in wx_copies:
        copy.wait_recv()
    for copy in wy_copies:
        copy.wait_recv()

    from_s = wgot[0]
    from_n = wgot[1]
    for k in range(CHUNKS):
        rows = pl.ds(k * ROWS, ROWS)
        for x in range(CX + 1):
            facex[x, rows, :] = (windx[x, rows, :] + windx[x + 1, rows, :]) * (1.0 / 120.0)
        behind = roll(from_s, 2 - k)
        ahead = roll(from_n, 3 - k)
        packed = jnp.where(low, facee[rows, :], ahead)
        facee[rows, :] = (roll(packed, 1) + packed) * (1.0 / 120.0)
        for x in range(CX):
            centre = windy[x, rows, :]
            halo = roll(behind, -(8 * x + 3))
            facey[x, rows, :] = (roll(jnp.where(lane == 127, halo, centre), 1) + centre) * (1.0 / 120.0)

    def section(sec, k, last):
        rows = rows_of(k)
        for pair in range(2):
            packs = []
            from_south, from_north = got_s[sec, k, pair], got_n[sec, k, pair]
            for part in range(2):
                s = 2 * pair + part
                mine = own[sec, s, rows, :]
                if part == 0:
                    before, after = from_south, roll(from_north, 3)
                else:
                    before, after = roll(from_south, -3), from_north
                merged = jnp.where(low, before, after)
                edge = jnp.where(low, mine, after)
                end = flux_terms(
                    roll(edge, 3), roll(edge, 2), roll(edge, 1), edge, roll(edge, -1), roll(edge, -2), facee[rows, :]
                )
                q = [field[sec, i, s, rows, :] for i in range(CX + 2 * H)]
                g = [q[i + 1] - q[i] for i in range(CX + 2 * H - 1)]
                d2 = {i: g[i] - g[i - 1] for i in range(1, CX + 2 * H - 1)}
                d3 = {i: d2[i + 1] - d2[i] for i in range(1, CX + 2 * H - 2)}
                d4 = {i: d3[i] - d3[i - 1] for i in range(2, CX + 2 * H - 2)}
                even = {i: (d4[i] - 5.0 * d2[i]) + 30.0 * q[i] for i in range(2, CX + 2 * H - 2)}
                flux = []
                for f in range(CX + 1):
                    speed = facex[f, rows, :]
                    flux.append(speed * (even[f + 2] + even[f + 3]) - jnp.abs(speed) * (d4[f + 3] - d4[f + 2]))
                packed = jnp.zeros((ROWS, LANES), jnp.float32)
                for x in range(CX):
                    c = q[H + x]
                    halo = roll(merged, -(8 * x + 3))
                    m1 = roll(jnp.where(lane >= 127, halo, c), 1)
                    m2 = roll(jnp.where(lane >= 126, halo, c), 2)
                    m3 = roll(jnp.where(lane >= 125, halo, c), 3)
                    p1 = roll(jnp.where(lane < 1, halo, c), -1)
                    p2 = roll(jnp.where(lane < 2, halo, c), -2)
                    across = flux_terms(m3, m2, m1, c, p1, p2, facey[x, rows, :])
                    ending = roll(end, -(8 * x + 3))
                    total = (flux[x + 1] - flux[x]) + (roll(jnp.where(lane == 0, ending, across), -1) - across)
                    base = field[0, H + x, s, rows, :]
                    new = base - square[sec, x] * total
                    if last:
                        result[x, s, rows, :] = new
                    else:
                        field[sec + 1, H + x, s, rows, :] = new
                        packed = jnp.where(slot == x, roll(new, 8 * x + 3), packed)
                if not last:
                    own[sec + 1, s, rows, :] = packed
                    packs.append(packed)
            if not last:
                pack_send(sec + 1, k, pair, *packs)

    def early(step, carry):
        sec, k = step // CHUNKS, lax.rem(step, CHUNKS)
        for copy in x_copies(sec, k) + y_copies(sec, k):
            copy.wait_recv()
        section(sec, k, False)
        for copy in x_copies(sec + 1, k) + y_copies(sec + 1, k):
            copy.start()
        return carry

    lax.fori_loop(0, 2 * CHUNKS, early, 0)

    def store(k):
        rows = rows_of(k)
        return pltpu.make_async_copy(result.at[:, :, rows, :], out.at[:, :, rows, :], store_o.at[k])

    def late(k, carry):
        for copy in x_copies(2, k) + y_copies(2, k):
            copy.wait_recv()
        section(2, k, True)
        store(k).start()
        return carry

    lax.fori_loop(0, CHUNKS, late, 0)

    for copy in wx_copies + wy_copies:
        copy.wait_send()

    def finish(step, carry):
        sec, k = step // CHUNKS, lax.rem(step, CHUNKS)
        for copy in x_copies(sec, k) + y_copies(sec, k):
            copy.wait_send()
        return carry

    lax.fori_loop(0, 3 * CHUNKS, finish, 0)

    def stored(k, carry):
        store(k).wait()
        return carry

    lax.fori_loop(0, CHUNKS, stored, 0)


def advance(scalars, winds, map_factor):
    f32 = jnp.float32
    dma = pltpu.SemaphoreType.DMA
    return pl.pallas_call(
        step_kernel,
        out_shape=jax.ShapeDtypeStruct((CX, NSC, LEV, LANES), f32),
        in_specs=[pl.BlockSpec(memory_space=pl.ANY)] * 3,
        out_specs=pl.BlockSpec(memory_space=pl.ANY),
        scratch_shapes=[
            pltpu.VMEM((3, CX + 2 * H, NSC, LEV, LANES), f32),
            pltpu.VMEM((CX + 2, LEV, LANES), f32),
            pltpu.VMEM((CX, LEV, LANES), f32),
            pltpu.VMEM((CX + 1, LEV, LANES), f32),
            pltpu.VMEM((CX, LEV, LANES), f32),
            pltpu.VMEM((LEV, LANES), f32),
            pltpu.VMEM((3, CX, ROWS, LANES), f32),
            pltpu.VMEM((3, NSC, LEV, LANES), f32),
            pltpu.VMEM((3, CHUNKS, 2, ROWS, LANES), f32),
            pltpu.VMEM((3, CHUNKS, 2, ROWS, LANES), f32),
            pltpu.VMEM((3, CHUNKS, 2, ROWS, LANES), f32),
            pltpu.VMEM((3, CHUNKS, 2, ROWS, LANES), f32),
            pltpu.VMEM((CX, NSC, LEV, LANES), f32),
            pltpu.VMEM((2, ROWS, LANES), f32),
            pltpu.VMEM((2, ROWS, LANES), f32),
            pltpu.VMEM((CX, LANES), f32),
            dma((NSC, CX)),
            dma((2, CX)),
            dma(()),
            dma((3, CHUNKS, 2)),
            dma((3, CHUNKS, 2)),
            dma((3, CHUNKS, 2)),
            dma((3, CHUNKS, 2)),
            dma((2,)),
            dma((2,)),
            dma((2,)),
            dma((2,)),
            dma((CHUNKS,)),
        ],
        compiler_params=pltpu.CompilerParams(collective_id=0, has_side_effects=True, vmem_limit_bytes=24 << 20),
        name="advance",
    )(scalars, winds, map_factor)


def urban_kernel(
    adv, counts, cols, classes, table, wall, indoor, out, wall_out, indoor_out, body, low_in, low_out, heat_pad, sem_in, sem_low, sem_out
):
    load_low = pltpu.make_async_copy(adv.at[:, 0, pl.ds(0, LOW), :], low_in, sem_in)
    load_low.start()
    rest = []
    for x in range(CX):
        rest.append(pltpu.make_async_copy(adv.at[x, 0, pl.ds(LOW, LEV - LOW), :], out.at[0, pl.ds(LOW, LEV - LOW), x, :], sem_out.at[0, x]))
        for s in range(1, NSC):
            rest.append(pltpu.make_async_copy(adv.at[x, s], out.at[s, :, x, :], sem_out.at[s, x]))
    for copy in rest:
        copy.start()
    slots = cols.shape[1]
    column = cols[...]
    col_x = column // LANES
    col_y = column % LANES
    live = lax.broadcasted_iota(jnp.int32, (1, slots), 1) < counts[0]
    onehot = (lax.broadcasted_iota(jnp.int32, (LANES, slots), 0) == col_y).astype(jnp.float32)
    ncls = table.shape[0]
    picked = (lax.broadcasted_iota(jnp.int32, (ncls, slots), 0) == classes[...]).astype(jnp.float32)
    areas = lax.dot_general(
        table[...], picked, (((0,), (0,)), ((), ())), precision=lax.Precision.HIGHEST, preferred_element_type=jnp.float32
    )
    load_low.wait()
    gathered = jnp.dot(
        low_in[...].reshape(CX * LOW, LANES), onehot, precision=lax.Precision.HIGHEST, preferred_element_type=jnp.float32
    ).reshape(CX, LOW, slots)
    air = jnp.zeros((LOW, slots), jnp.float32)
    for x in range(CX):
        air = jnp.where(col_x == x, gathered[x], air)
    walls = wall[...]
    room = indoor[...]
    top = walls[0:1]
    heat = heat_coef * areas * (top - air[:UL])
    first = top - wall_coef * jnp.sum(heat, axis=0, keepdims=True) + conduct * (walls[1:2] - top)
    middle = walls[1:-1] + conduct * (walls[:-2] - 2.0 * walls[1:-1] + walls[2:])
    bottom = walls[NWL - 1 : NWL]
    last = bottom + conduct * (walls[NWL - 2 : NWL - 1] - bottom) + inner_coef * (room - bottom)
    wall_out[0:1] = jnp.where(live, first, top)
    wall_out[1 : NWL - 1] = jnp.where(live, middle, walls[1:-1])
    wall_out[NWL - 1 : NWL] = jnp.where(live, last, bottom)
    indoor_out[...] = jnp.where(live, room + room_coef * (bottom - room), room)
    heat_pad[...] = jnp.zeros_like(heat_pad)
    heat_pad[0:UL] = jnp.where(live, flux_coef * heat, 0.0)
    padded = heat_pad[...]
    for x in range(CX):
        body[x] = jnp.where(col_x == x, padded, 0.0)
    spread = lax.dot_general(
        body[...].reshape(CX * LOW, slots), onehot, (((1,), (1,)), ((), ())),
        precision=lax.Precision.HIGHEST, preferred_element_type=jnp.float32,
    )
    low_out[...] = low_in[...] + spread.reshape(CX, LOW, LANES)
    final = [pltpu.make_async_copy(low_out.at[x], out.at[0, pl.ds(0, LOW), x, :], sem_low.at[x]) for x in range(CX)]
    for copy in final:
        copy.start()
    for copy in rest + final:
        copy.wait()


def urban(adv, counts, cols, classes, table, wall, indoor):
    f32 = jnp.float32
    slots = wall.shape[1]
    vmem = pl.BlockSpec(memory_space=pltpu.VMEM)
    anywhere = pl.BlockSpec(memory_space=pl.ANY)
    dma = pltpu.SemaphoreType.DMA
    return pl.pallas_call(
        urban_kernel,
        out_shape=(
            jax.ShapeDtypeStruct((NSC, LEV, CX, LANES), f32),
            jax.ShapeDtypeStruct((NWL, slots), f32),
            jax.ShapeDtypeStruct((1, slots), f32),
        ),
        in_specs=[anywhere, pl.BlockSpec(memory_space=pltpu.SMEM)] + [vmem] * 5,
        out_specs=(anywhere, vmem, vmem),
        scratch_shapes=[
            pltpu.VMEM((CX, LOW, slots), f32),
            pltpu.VMEM((CX, LOW, LANES), f32),
            pltpu.VMEM((CX, LOW, LANES), f32),
            pltpu.VMEM((LOW, slots), f32),
            dma(()),
            dma((CX,)),
            dma((NSC, CX)),
        ],
        compiler_params=pltpu.CompilerParams(vmem_limit_bytes=16 << 20),
        name="urban",
    )(adv, counts, cols.reshape(1, slots), classes.reshape(1, slots), table, wall, indoor.reshape(1, slots))


def per_device(scalars, winds, map_factor, urban_counts, urban_cols, street_class, area_table, wall_temp, indoor_temp):
    adv = advance(scalars, winds, map_factor)
    scalars_out, wall_out, indoor_out = urban(
        adv, urban_counts, urban_cols, street_class, area_table, wall_temp, indoor_temp
    )
    return (scalars_out, wall_out, indoor_out.reshape(indoor_temp.shape))


def solution(mesh):
    in_specs = (
        P(None, None, "gx", "gy"),
        P(None, None, "gx", "gy"),
        P("gx", "gy"),
        P(("gx", "gy")),
        P(("gx", "gy")),
        P(("gx", "gy")),
        P(),
        P(None, ("gx", "gy")),
        P(("gx", "gy")),
    )
    out_specs = (P(None, None, "gx", "gy"), P(None, ("gx", "gy")), P(("gx", "gy")))
    return jax.shard_map(per_device, mesh=mesh, in_specs=in_specs, out_specs=out_specs, check_vma=False)
```

profile of v0, /device:TPU:0, one launch (start us, length us, event | category | flops | bytes accessed | tf_op | source)
XLA Modules:
  0.0 85.7 jit_solution(10997914852077322005)
XLA Ops:
  1.3 0.0 copy-start
  1.3 1.6 %copy-done = f32[4,64,16,128]{3,2,1,0:T(8,128)S(1)} copy-done((f32[4,64,16,128]{3,2,1,0:T(8,128)S(1)}, f32[4,64,16,128]{3,2,1,0:T(8,128)}, u32[]{:S(2)}) %copy-start) | copy-done | bytes 2097176
  2.9 0.0 copy-start.1
  2.9 1.2 %copy-done.1 = f32[2,64,16,128]{3,2,1,0:T(8,128)S(1)} copy-done((f32[2,64,16,128]{3,2,1,0:T(8,128)S(1)}, f32[2,64,16,128]{3,2,1,0:T(8,128)}, u32[]{:S(2)}) %copy-start.1) | copy-done | bytes 1048600
  4.1 0.0 copy-start.3
  4.1 0.7 copy-done.3
  4.8 0.0 copy-start.2
  4.8 0.0 copy-start.4
  4.8 0.0 copy-start.5
  4.8 0.0 copy-start.6
  4.8 0.0 copy-start.7
  4.8 76.7 %advance.1.adv = f32[16,4,64,128]{3,2,1,0:T(8,128)S(1)} custom-call(f32[4,64,16,128]{3,2,1,0:T(8,128)S(1)} %copy-done, f32[2,64,16,128]{3,2,1,0:T(8,128)S(1)} %copy-done.1, f32[16,128]{1,0:T(8,128)S(1)} %copy-done.3), custom_call_target="tpu_custom_call" | custom-call | tf_op jit(solution)/shard_map/advance/pallas_call | solution.py:297
  81.5 0.0 copy-done.2
  81.5 0.0 copy-done.4
  81.5 0.0 copy-done.5
  81.5 0.0 copy-done.6
  81.5 0.0 copy-done.7
  81.5 4.2 %urban.1 = (f32[4,64,16,128]{3,2,1,0:T(8,128)}, f32[10,1024]{1,0:T(8,128)}, f32[1,1024]{1,0:T(1,128)}) custom-call(f32[16,4,64,128]{3,2,1,0:T(8,128)S(1)} %advance.1.adv, s32[1]{0:T(128)S(6)} %copy.12.counts, s32[1,1024]{1,0:T(1,128)S(1)} %bitcast.4, s32[1,1024]{1,0:T(1,128)S(1)} %bitcast.5, f32[10,10]{1,0:T(8,128)S(1)} %copy-done.4, ...), custom_call_target="tpu_custom_call" | custom-call | tf_op jit(solution)/shard_map/urban/pallas_call | solution.py:402
Async XLA Ops:
  1.3 1.6 %copy-start = (f32[4,64,16,128]{3,2,1,0:T(8,128)S(1)}, f32[4,64,16,128]{3,2,1,0:T(8,128)}, u32[]{:S(2)}) copy-start(f32[4,64,16,128]{3,2,1,0:T(8,128)} %scal.1) | copy-start | bytes 6291460
  2.9 1.2 %copy-start.1 = (f32[2,64,16,128]{3,2,1,0:T(8,128)S(1)}, f32[2,64,16,128]{3,2,1,0:T(8,128)}, u32[]{:S(2)}) copy-start(f32[2,64,16,128]{3,2,1,0:T(8,128)} %wind.1) | copy-start | bytes 3145732
  4.1 0.7 copy-start.3
  4.8 76.7 %copy-start.2 = (f32[10,1024]{1,0:T(8,128)S(1)}, f32[10,1024]{1,0:T(8,128)}, u32[]{:S(2)}) copy-start(f32[10,1024]{1,0:T(8,128)} %wall.1) | copy-start | bytes 122884
  4.8 76.7 %copy-start.4 = (f32[10,10]{1,0:T(8,128)S(1)}, f32[10,10]{1,0:T(8,128)}, u32[]{:S(2)}) copy-start(f32[10,10]{1,0:T(8,128)} %table.1) | copy-start | bytes 1204
  4.8 76.7 %copy-start.5 = (s32[1024]{0:T(1024)S(1)}, s32[1024]{0:T(1024)}, u32[]{:S(2)}) copy-start(s32[1024]{0:T(1024)} %param.13) | copy-start | bytes 12292
  4.8 76.7 %copy-start.6 = (s32[1024]{0:T(1024)S(1)}, s32[1024]{0:T(1024)}, u32[]{:S(2)}) copy-start(s32[1024]{0:T(1024)} %param.14) | copy-start | bytes 12292
  4.8 76.7 %copy-start.7 = (f32[1024]{0:T(1024)S(1)}, f32[1024]{0:T(1024)}, u32[]{:S(2)}) copy-start(f32[1024]{0:T(1024)} %param.17) | copy-start | bytes 12292
where the time goes:
time: 85.9 us; the launch traced here: 85.7 us
  Pallas kernels  80.8 us (94%)
  local copies, waits for them, and re-layouts  3.52 us (4%)
  between operations  1.35 us (2%)
    pallas_call x1, Pallas kernels, advance(): pl.pallas_call(step_kernel, out_shape=jax.ShapeDtypeStruct((CX, NSC, LEV,...  76.7 us
    pallas_call x1, Pallas kernels, urban(): pl.pallas_call(urban_kernel, out_shape=(jax.ShapeDtypeStruct((NSC, LEV, C...  4.16 us
    unnamed x16, local copies, waits for them, and re-layouts  3.52 us

commit v1 on v0

--- a/solution.py
+++ b/solution.py
@@ -32,15 +32,31 @@
     return pltpu.roll(value, shift % LANES, 1)
 
 
-def flux_terms(m3, m2, m1, q, p1, p2, speed):
-    even = 37.0 * (m1 + q) - 8.0 * (m2 + p1) + (m3 + p2)
-    odd = (p2 - m3) - 5.0 * (p1 - m2) + 10.0 * (q - m1)
-    return speed * even - jnp.abs(speed) * odd
+def split(value):
+    high = value.astype(jnp.bfloat16)
+    return high, (value - high.astype(jnp.float32)).astype(jnp.bfloat16)
+
+
+def fill_stencil(stencil):
+    row = lax.broadcasted_iota(jnp.int32, (LANES, LANES), 0)
+    column = lax.broadcasted_iota(jnp.int32, (LANES, LANES), 1)
+    halo = jnp.where(row >= LANES - H, row - LANES, jnp.where(row < H, row + LANES, 4 * LANES))
+    for source, cell in enumerate((row, halo)):
+        for block in range(4):
+            offset = cell - column + (2 if block < 2 else 3)
+            weights = (1.0, -8.0, 37.0, 37.0, -8.0, 1.0) if block % 2 == 0 else (-1.0, 5.0, -10.0, 10.0, -5.0, 1.0)
+            band = jnp.zeros((LANES, LANES), jnp.float32)
+            for at, weight in enumerate(weights):
+                band = jnp.where(offset == at, weight, band)
+            band = band.astype(jnp.bfloat16)
+            for part in range(2):
+                stencil[pl.ds((2 * source + part) * LANES, LANES), pl.ds(block * LANES, LANES)] = band
 
 
 def step_kernel(
     scal, wind, mapf, out,
-    field, windx, windy, facex, facey, facee, square, own, give_n, give_s, got_s, got_n, result, wpack, wgot, mapbuf,
+    field, windx, windy, facex, facex_abs, face_r, face_r_abs, face_l, face_l_abs, square, give_n, give_s, got_s, got_n,
+    result, wpack, wgot, mapbuf, stencil, cells, across,
     load_s, load_w, load_m, sx, rx, sy, ry, swx, rwx, swy, rwy, store_o,
 ):
     gx, gy = lax.axis_index("gx"), lax.axis_index("gy")
@@ -106,6 +122,7 @@
         remote(wpack.at[1], wgot.at[1], swy.at[1], rwy.at[1], south),
     )
 
+    fill_stencil(stencil)
     for s in range(NSC):
         for x in EDGE_X:
             load_scalar(s, x).wait()
@@ -141,7 +158,6 @@
             packed = jnp.where(slot == x, roll(windy[x, pl.ds(k * ROWS, ROWS), :], 8 * x + 3), packed)
         to_n = jnp.where(inside == k, roll(packed, k - 2), to_n)
         to_s = jnp.where(inside == k, roll(packed, k - 3), to_s)
-        facee[pl.ds(k * ROWS, ROWS), :] = packed
     wpack[0] = to_n
     wpack[1] = to_s
     for copy in wy_copies:
@@ -159,7 +175,6 @@
                 packed = jnp.zeros((ROWS, LANES), jnp.float32)
                 for x in range(CX):
                     packed = jnp.where(slot == x, roll(field[0, H + x, s, rows, :], 8 * x + 3), packed)
-                own[0, s, rows, :] = packed
                 packs.append(packed)
             pack_send(0, k, pair, *packs)
         for copy in y_copies(0, k):
@@ -187,67 +202,76 @@
     for k in range(CHUNKS):
         rows = pl.ds(k * ROWS, ROWS)
         for x in range(CX + 1):
-            facex[x, rows, :] = (windx[x, rows, :] + windx[x + 1, rows, :]) * (1.0 / 120.0)
-        behind = roll(from_s, 2 - k)
-        ahead = roll(from_n, 3 - k)
-        packed = jnp.where(low, facee[rows, :], ahead)
-        facee[rows, :] = (roll(packed, 1) + packed) * (1.0 / 120.0)
+            speed = (windx[x, rows, :] + windx[x + 1, rows, :]) * (1.0 / 120.0)
+            facex[x, rows, :] = speed
+            facex_abs[x, rows, :] = jnp.abs(speed)
+        merged = jnp.where(low, roll(from_s, 2 - k), roll(from_n, 3 - k))
         for x in range(CX):
             centre = windy[x, rows, :]
-            halo = roll(behind, -(8 * x + 3))
-            facey[x, rows, :] = (roll(jnp.where(lane == 127, halo, centre), 1) + centre) * (1.0 / 120.0)
+            halo = roll(merged, -(8 * x + 3))
+            left = (roll(jnp.where(lane == LANES - 1, halo, centre), 1) + centre) * (1.0 / 120.0)
+            right = (roll(jnp.where(lane == 0, halo, centre), -1) + centre) * (1.0 / 120.0)
+            face_l[x, rows, :] = left
+            face_l_abs[x, rows, :] = jnp.abs(left)
+            face_r[x, rows, :] = right
+            face_r_abs[x, rows, :] = jnp.abs(right)
+
+    size = NSC * ROWS
+    half = CX // 2
 
     def section(sec, k, last):
         rows = rows_of(k)
+        merged = []
         for pair in range(2):
-            packs = []
             from_south, from_north = got_s[sec, k, pair], got_n[sec, k, pair]
-            for part in range(2):
-                s = 2 * pair + part
-                mine = own[sec, s, rows, :]
-                if part == 0:
-                    before, after = from_south, roll(from_north, 3)
-                else:
-                    before, after = roll(from_south, -3), from_north
-                merged = jnp.where(low, before, after)
-                edge = jnp.where(low, mine, after)
-                end = flux_terms(
-                    roll(edge, 3), roll(edge, 2), roll(edge, 1), edge, roll(edge, -1), roll(edge, -2), facee[rows, :]
-                )
-                q = [field[sec, i, s, rows, :] for i in range(CX + 2 * H)]
-                g = [q[i + 1] - q[i] for i in range(CX + 2 * H - 1)]
-                d2 = {i: g[i] - g[i - 1] for i in range(1, CX + 2 * H - 1)}
-                d3 = {i: d2[i + 1] - d2[i] for i in range(1, CX + 2 * H - 2)}
-                d4 = {i: d3[i] - d3[i - 1] for i in range(2, CX + 2 * H - 2)}
-                even = {i: (d4[i] - 5.0 * d2[i]) + 30.0 * q[i] for i in range(2, CX + 2 * H - 2)}
-                flux = []
-                for f in range(CX + 1):
-                    speed = facex[f, rows, :]
-                    flux.append(speed * (even[f + 2] + even[f + 3]) - jnp.abs(speed) * (d4[f + 3] - d4[f + 2]))
-                packed = jnp.zeros((ROWS, LANES), jnp.float32)
-                for x in range(CX):
-                    c = q[H + x]
-                    halo = roll(merged, -(8 * x + 3))
-                    m1 = roll(jnp.where(lane >= 127, halo, c), 1)
-                    m2 = roll(jnp.where(lane >= 126, halo, c), 2)
-                    m3 = roll(jnp.where(lane >= 125, halo, c), 3)
-                    p1 = roll(jnp.where(lane < 1, halo, c), -1)
-                    p2 = roll(jnp.where(lane < 2, halo, c), -2)
-                    across = flux_terms(m3, m2, m1, c, p1, p2, facey[x, rows, :])
-                    ending = roll(end, -(8 * x + 3))
-                    total = (flux[x + 1] - flux[x]) + (roll(jnp.where(lane == 0, ending, across), -1) - across)
-                    base = field[0, H + x, s, rows, :]
-                    new = base - square[sec, x] * total
+            merged.append(jnp.where(low, from_south, roll(from_north, 3)))
+            merged.append(jnp.where(low, roll(from_south, -3), from_north))
+        merged = jnp.concatenate(merged, axis=0)
+        for part in range(2):
+            for x in range(part * half, (part + 1) * half):
+                at = pl.ds(x * size, size)
+                high, rest = split(field[sec, H + x, :, rows, :].reshape(size, LANES))
+                cells[at, 0:LANES] = high
+                cells[at, LANES : 2 * LANES] = rest
+                high, rest = split(roll(merged, -(8 * x + 3)))
+                cells[at, 2 * LANES : 3 * LANES] = high
+                cells[at, 3 * LANES : 4 * LANES] = rest
+            at = pl.ds(part * half * size, half * size)
+            across[at, :] = jnp.dot(cells[at, :], stencil[...], preferred_element_type=jnp.float32)
+        packs = []
+        for s in range(NSC):
+            packed = jnp.zeros((ROWS, LANES), jnp.float32)
+            q, g, d2, d3, d4, even, flux = {}, {}, {}, {}, {}, {}, {}
+            for i in range(CX + 2 * H):
+                q[i] = field[sec, i, s, rows, :]
+                if i >= 1:
+                    g[i - 1] = q[i] - q[i - 1]
+                if i >= 2:
+                    d2[i - 1] = g[i - 1] - g[i - 2]
+                if i >= 3:
+                    d3[i - 2] = d2[i - 1] - d2[i - 2]
+                if i >= 4:
+                    d4[i - 2] = d3[i - 2] - d3[i - 3]
+                    even[i - 2] = (d4[i - 2] - 5.0 * d2[i - 2]) + 30.0 * q[i - 2]
+                if i >= 5:
+                    f = i - 5
+                    flux[f] = facex[f, rows, :] * (even[i - 3] + even[i - 2]) - facex_abs[f, rows, :] * (d4[i - 2] - d4[i - 3])
+                if i >= 6:
+                    x = i - 6
+                    at = pl.ds(x * size + s * ROWS, ROWS)
+                    total = flux[x + 1] - flux[x]
+                    total += face_r[x, rows, :] * across[at, 0:LANES] - face_r_abs[x, rows, :] * across[at, LANES : 2 * LANES]
+                    total -= face_l[x, rows, :] * across[at, 2 * LANES : 3 * LANES] - face_l_abs[x, rows, :] * across[at, 3 * LANES : 4 * LANES]
+                    new = field[0, H + x, s, rows, :] - square[sec, x] * total
                     if last:
                         result[x, s, rows, :] = new
                     else:
                         field[sec + 1, H + x, s, rows, :] = new
                         packed = jnp.where(slot == x, roll(new, 8 * x + 3), packed)
-                if not last:
-                    own[sec + 1, s, rows, :] = packed
-                    packs.append(packed)
-            if not last:
-                pack_send(sec + 1, k, pair, *packs)
+            packs.append(packed)
+        if not last:
+            for pair in range(2):
+                pack_send(sec + 1, k, pair, packs[2 * pair], packs[2 * pair + 1])
 
     def early(step, carry):
         sec, k = step // CHUNKS, lax.rem(step, CHUNKS)
@@ -297,17 +321,19 @@
     return pl.pallas_call(
         step_kernel,
         out_shape=jax.ShapeDtypeStruct((CX, NSC, LEV, LANES), f32),
-        in_specs=[pl.BlockSpec(memory_space=pl.ANY)] * 3,
+        in_specs=[pl.BlockSpec(memory_space=pltpu.HBM)] * 3,
         out_specs=pl.BlockSpec(memory_space=pl.ANY),
         scratch_shapes=[
             pltpu.VMEM((3, CX + 2 * H, NSC, LEV, LANES), f32),
             pltpu.VMEM((CX + 2, LEV, LANES), f32),
             pltpu.VMEM((CX, LEV, LANES), f32),
             pltpu.VMEM((CX + 1, LEV, LANES), f32),
+            pltpu.VMEM((CX + 1, LEV, LANES), f32),
             pltpu.VMEM((CX, LEV, LANES), f32),
-            pltpu.VMEM((LEV, LANES), f32),
+            pltpu.VMEM((CX, LEV, LANES), f32),
+            pltpu.VMEM((CX, LEV, LANES), f32),
+            pltpu.VMEM((CX, LEV, LANES), f32),
             pltpu.VMEM((3, CX, ROWS, LANES), f32),
-            pltpu.VMEM((3, NSC, LEV, LANES), f32),
             pltpu.VMEM((3, CHUNKS, 2, ROWS, LANES), f32),
             pltpu.VMEM((3, CHUNKS, 2, ROWS, LANES), f32),
             pltpu.VMEM((3, CHUNKS, 2, ROWS, LANES), f32),
@@ -316,6 +342,9 @@
             pltpu.VMEM((2, ROWS, LANES), f32),
             pltpu.VMEM((2, ROWS, LANES), f32),
             pltpu.VMEM((CX, LANES), f32),
+            pltpu.VMEM((4 * LANES, 4 * LANES), jnp.bfloat16),
+            pltpu.VMEM((CX * NSC * ROWS, 4 * LANES), jnp.bfloat16),
+            pltpu.VMEM((CX * NSC * ROWS, 4 * LANES), f32),
             dma((NSC, CX)),
             dma((2, CX)),
             dma(()),
@@ -329,7 +358,7 @@
             dma((2,)),
             dma((CHUNKS,)),
         ],
-        compiler_params=pltpu.CompilerParams(collective_id=0, has_side_effects=True, vmem_limit_bytes=24 << 20),
+        compiler_params=pltpu.CompilerParams(collective_id=0, has_side_effects=True, vmem_limit_bytes=58 << 20),
         name="advance",
     )(scalars, winds, map_factor)
 

time: 85.9 us -> 54.8 us (0.64)
  Pallas kernels: 80.8 us -> 51.6 us
  local copies, waits for them, and re-layouts: 3.52 us -> 1.61 us
    pallas_call x1, Pallas kernels: 76.7 us -> 47.5 us  [advance(): pl.pallas_call(step_kernel, out_shape=jax.ShapeDtypeStruct((CX, NSC, LEV,...]
    unnamed x16 -> x12, local copies, waits for them, and re-layouts: 3.52 us -> 1.61 us
where the time goes in v1:
time: 54.8 us; the launch traced here: 54.6 us
  Pallas kernels  51.6 us (94%)
  local copies, waits for them, and re-layouts  1.61 us (3%)
  between operations  1.37 us (2%)
    pallas_call x1, Pallas kernels, advance(): pl.pallas_call(step_kernel, out_shape=jax.ShapeDtypeStruct((CX, NSC, LEV,...  47.5 us
    pallas_call x1, Pallas kernels, urban(): pl.pallas_call(urban_kernel, out_shape=(jax.ShapeDtypeStruct((NSC, LEV, C...  4.15 us
    unnamed x12, local copies, waits for them, and re-layouts  1.61 us

profile of v1, /device:TPU:0, one launch (start us, length us, event | category | flops | bytes accessed | tf_op | source)
XLA Modules:
  0.0 54.6 jit_solution(2404950911130547918)
XLA Ops:
  1.3 0.0 copy-start.1
  1.3 0.0 copy-start.2
  1.3 0.0 copy-start.3
  1.3 0.0 copy-start.4
  1.3 0.0 copy-start.5
  1.3 47.5 %advance.1.adv = f32[16,4,64,128]{3,2,1,0:T(8,128)} custom-call(f32[4,64,16,128]{3,2,1,0:T(8,128)} %scal.1, f32[2,64,16,128]{3,2,1,0:T(8,128)} %wind.1, f32[16,128]{1,0:T(8,128)} %mapf.1), custom_call_target="tpu_custom_call" | custom-call | tf_op jit(solution)/shard_map/advance/pallas_call | solution.py:321
  48.8 0.0 copy-done.1
  48.8 0.0 copy-done.2
  48.8 0.0 copy-done.3
  48.8 0.0 copy-done.4
  48.8 0.0 copy-done.5
  48.8 0.0 copy-start
  48.9 1.6 %copy-done = f32[16,4,64,128]{3,2,1,0:T(8,128)S(1)} copy-done((f32[16,4,64,128]{3,2,1,0:T(8,128)S(1)}, f32[16,4,64,128]{3,2,1,0:T(8,128)}, u32[]{:S(2)}) %copy-start) | copy-done | bytes 2097176
  50.4 4.2 %urban.1 = (f32[4,64,16,128]{3,2,1,0:T(8,128)}, f32[10,1024]{1,0:T(8,128)}, f32[1,1024]{1,0:T(1,128)}) custom-call(f32[16,4,64,128]{3,2,1,0:T(8,128)S(1)} %copy-done, s32[1]{0:T(128)S(6)} %copy.12.counts, s32[1,1024]{1,0:T(1,128)S(1)} %bitcast.4, s32[1,1024]{1,0:T(1,128)S(1)} %bitcast.5, f32[10,10]{1,0:T(8,128)S(1)} %copy-done.2, f32[10,1024]{1,0:T(8,128)S(1)} %copy-done.1, ...), custom_call_target="tpu_custom_call" | custom-call | tf_op jit(solution)/shard_map/urban/pallas_call | solution.py:431
Async XLA Ops:
  1.3 47.5 %copy-start.1 = (f32[10,1024]{1,0:T(8,128)S(1)}, f32[10,1024]{1,0:T(8,128)}, u32[]{:S(2)}) copy-start(f32[10,1024]{1,0:T(8,128)} %wall.1) | copy-start | bytes 122884
  1.3 47.5 %copy-start.2 = (f32[10,10]{1,0:T(8,128)S(1)}, f32[10,10]{1,0:T(8,128)}, u32[]{:S(2)}) copy-start(f32[10,10]{1,0:T(8,128)} %table.1) | copy-start | bytes 1204
  1.3 47.5 %copy-start.3 = (s32[1024]{0:T(1024)S(1)}, s32[1024]{0:T(1024)}, u32[]{:S(2)}) copy-start(s32[1024]{0:T(1024)} %param.13) | copy-start | bytes 12292
  1.3 47.5 %copy-start.4 = (s32[1024]{0:T(1024)S(1)}, s32[1024]{0:T(1024)}, u32[]{:S(2)}) copy-start(s32[1024]{0:T(1024)} %param.14) | copy-start | bytes 12292
  1.3 47.5 %copy-start.5 = (f32[1024]{0:T(1024)S(1)}, f32[1024]{0:T(1024)}, u32[]{:S(2)}) copy-start(f32[1024]{0:T(1024)} %param.17) | copy-start | bytes 12292
  48.8 1.6 %copy-start = (f32[16,4,64,128]{3,2,1,0:T(8,128)S(1)}, f32[16,4,64,128]{3,2,1,0:T(8,128)}, u32[]{:S(2)}) copy-start(f32[16,4,64,128]{3,2,1,0:T(8,128)} %advance.1.adv) | copy-start | bytes 6291460
